TPU v7x, 32 devices: a whole 2x2x4 slice. The times are simulated.
32 devices in a mesh: ctx: 4 (over y, x), dp: 8 (over z, core).
Axes of the slice: x: 2, y: 2, z: 4, core: 2. Of those that a mesh axis runs over, the one named last changes fastest.
Arguments:
- queries: bfloat16 [8, 512, 1024], P('dp', 'ctx'), may hold values from -6 to 6
- keys_in: bfloat16 [8, 512, 256], P('dp', 'ctx'), may hold values from -6 to 6
- values_in: bfloat16 [8, 512, 256], P('dp', 'ctx'), may hold values from -6 to 6
- patch_order: int32 [8, 4, 128], P('dp', 'ctx'), may hold values from 0 to 127, each once within a row
- block_mask: int32 [8, 16, 8], P('dp', 'ctx'), may hold values 0 or 1
- out_weight: bfloat16 [1024, 1024], P('dp'), may hold values from -0.1875 to 0.1875
- cotangent: bfloat16 [8, 512, 1024], P('dp', 'ctx'), may hold values from -6 to 6
Outputs:
- mixed: bfloat16 [8, 512, 1024], P('dp', 'ctx')
- grad_queries: bfloat16 [8, 512, 1024], P('dp', 'ctx')
- grad_keys: bfloat16 [8, 512, 256], P('dp', 'ctx')
- grad_values: bfloat16 [8, 512, 256], P('dp', 'ctx')
- grad_weight: float32 [1024, 1024], P('dp', 'ctx')
Inputs may be any that keep to these rules, and one draw needn't show every extreme that they name: `patch_order`: each row of 128 entries is a permutation.
All inputs are finite; a program needn't handle non-finite values. No bound on the sum of `block_mask` on one device may be relied on, other than what follows from the above.
Results may differ from a plain program's by a relative error of at most 0.015.
Values may be sent and summed in bfloat16 or wider, within the bound.
No kernel may reach another device: no remote copies, remote signals or barrier semaphores. Data moves between devices by JAX's collectives and lax.ppermute only.
A program may use at most 64 MiB of HBM per device.

v0:
```python
import math
import jax
import jax.numpy as jnp
from jax import lax
from jax.sharding import PartitionSpec as P

QUERY_HEADS = 8
KEY_VALUE_HEADS = 2
HEAD_WIDTH = 128
BLK = 32


def with_halo(block, sides, width):
    for axis, dim in sides:
        count = lax.axis_size(axis)
        forward = [(i, i + 1) for i in range(count - 1)]
        forward.append((count - 1, 0))
        backward = [(target, source) for source, target in forward]
        low = lax.ppermute(
            lax.slice_in_dim(block, block.shape[dim] - width, None, axis=dim), axis, forward
        )
        high = lax.ppermute(lax.slice_in_dim(block, 0, width, axis=dim), axis, backward)
        block = jnp.concatenate([low, block, high], axis=dim)
    return block


def shards(queries, keys_in, values_in, patch_order, block_mask, out_weight, cotangent):
    scale = 1.0 / math.sqrt(HEAD_WIDTH)
    query_group = QUERY_HEADS // KEY_VALUE_HEADS
    token_rows = queries.shape[1]
    key_head_width = keys_in.shape[2]
    row_position = patch_order[0, 0]
    query_sequence = jnp.take(queries[0], row_position, axis=0)
    key_sequence = jnp.take(keys_in[0], row_position, axis=0)
    value_sequence = jnp.take(values_in[0], row_position, axis=0)
    dy_seq = jnp.take(cotangent[0], row_position, axis=0)
    kv_pair = jnp.concatenate([key_sequence, value_sequence], axis=1)
    neighbour_band = with_halo(kv_pair, (("ctx", 0),), token_rows)
    key_band = neighbour_band[:, :key_head_width].reshape(
        3 * token_rows, KEY_VALUE_HEADS, HEAD_WIDTH
    )
    value_band = neighbour_band[:, key_head_width:].reshape(
        3 * token_rows, KEY_VALUE_HEADS, HEAD_WIDTH
    )
    weight_all = lax.all_gather(out_weight, "dp", axis=0, tiled=True)
    expanded = jnp.repeat(jnp.repeat(block_mask[0], BLK, 0), BLK, 1) > 0
    allowed = jnp.concatenate(
        [
            expanded[:, :token_rows],
            jnp.ones((token_rows, token_rows), bool),
            expanded[:, token_rows:],
        ],
        1,
    )
    allowed = allowed[None, None]
    query_four = query_sequence.reshape(token_rows, KEY_VALUE_HEADS, query_group, HEAD_WIDTH)
    scores = (
        jnp.einsum("tkgd,skd->kgts", query_four, key_band, preferred_element_type=jnp.float32)
        * scale
    )
    scores = jnp.where(allowed, scores, -1e30)
    highest = jnp.max(scores, axis=-1, keepdims=True)
    weights = jnp.where(allowed, jnp.exp(scores - highest), 0.0)
    probs = weights / jnp.sum(weights, axis=-1, keepdims=True)
    probs_b = probs.astype(jnp.bfloat16)
    attended_f = jnp.einsum(
        "kgts,skd->tkgd", probs_b, value_band, preferred_element_type=jnp.float32
    )
    attended = attended_f.astype(jnp.bfloat16).reshape(token_rows, query_sequence.shape[1])
    mixed_seq = jnp.dot(attended, weight_all, preferred_element_type=jnp.float32).astype(
        jnp.bfloat16
    )
    mixed_out = jnp.zeros_like(mixed_seq).at[row_position].set(mixed_seq)
    attention_gradient = lax.dot_general(
        dy_seq, weight_all, (((1,), (1,)), ((), ())), preferred_element_type=jnp.float32
    ).astype(jnp.bfloat16)
    attention_gradient4 = attention_gradient.reshape(
        token_rows, KEY_VALUE_HEADS, query_group, HEAD_WIDTH
    )
    d_probs = jnp.einsum(
        "tkgd,skd->kgts", attention_gradient4, value_band, preferred_element_type=jnp.float32
    )
    delta = jnp.sum(attention_gradient4.astype(jnp.float32) * attended_f, axis=-1)
    delta = jnp.transpose(delta, (1, 2, 0))[..., None]
    d_scores_b = (probs * (d_probs - delta)).astype(jnp.bfloat16)
    grad_q_seq = (
        jnp.einsum("kgts,skd->tkgd", d_scores_b, key_band, preferred_element_type=jnp.float32)
        * scale
    ).astype(jnp.bfloat16)
    grad_q_out = (
        jnp.zeros_like(query_sequence)
        .at[row_position]
        .set(grad_q_seq.reshape(token_rows, query_sequence.shape[1]))
    )
    part_k = (
        jnp.einsum("kgts,tkgd->skd", d_scores_b, query_four, preferred_element_type=jnp.float32)
        * scale
    ).astype(jnp.bfloat16)
    part_v = jnp.einsum(
        "kgts,tkgd->skd", probs_b, attention_gradient4, preferred_element_type=jnp.float32
    ).astype(jnp.bfloat16)
    part_both = jnp.concatenate(
        [
            part_k.reshape(3 * token_rows, key_head_width),
            part_v.reshape(3 * token_rows, key_head_width),
        ],
        axis=1,
    )
    outgoing = jnp.concatenate([part_both[:token_rows], part_both[2 * token_rows :]], axis=0)
    arrived = with_halo(outgoing, (("ctx", 0),), token_rows)
    summed = (
        part_both[token_rows : 2 * token_rows].astype(jnp.float32)
        + arrived[:token_rows].astype(jnp.float32)
        + arrived[3 * token_rows :].astype(jnp.float32)
    )
    summed = summed.astype(jnp.bfloat16)
    grad_k_out = jnp.zeros_like(key_sequence).at[row_position].set(summed[:, :key_head_width])
    grad_v_out = jnp.zeros_like(value_sequence).at[row_position].set(summed[:, key_head_width:])
    total_tokens = lax.axis_size("dp") * token_rows * lax.axis_size("ctx")
    norm_factor = 1.0 / math.sqrt(total_tokens)
    tile_rows = lax.psum_scatter(
        lax.dot_general(
            dy_seq, attended, (((0,), (0,)), ((), ())), preferred_element_type=jnp.float32
        ).astype(jnp.bfloat16),
        "ctx",
        scatter_dimension=0,
        tiled=True,
    ).astype(jnp.float32)
    grad_weight = lax.psum_scatter(tile_rows, "dp", scatter_dimension=1, tiled=True).T * norm_factor
    return (mixed_out[None], grad_q_out[None], grad_k_out[None], grad_v_out[None], grad_weight)


def solution(mesh):
    in_specs = (
        P("dp", "ctx", None),
        P("dp", "ctx", None),
        P("dp", "ctx", None),
        P("dp", "ctx", None),
        P("dp", "ctx", None),
        P("dp", None),
        P("dp", "ctx", None),
    )
    out_specs = (
        P("dp", "ctx", None),
        P("dp", "ctx", None),
        P("dp", "ctx", None),
        P("dp", "ctx", None),
        P("dp", "ctx"),
    )
    return jax.shard_map(shards, mesh=mesh, in_specs=in_specs, out_specs=out_specs, check_vma=False)
```

profile of v0, /device:TPU:0, one launch (start us, length us, event | category | flops | bytes accessed | tf_op | source)
XLA Modules:
  0.0 127.7 jit_solution(1401333764290365833)
XLA Ops:
  7.2 0.0 copy-start
  7.2 0.0 copy-start.10
  7.2 0.0 all-gather.2.cloned.1.call-start
  7.2 0.7 all-gather.2.cloned.1.call-update
  7.9 0.0 reduce-scatter.3.cloned.1.call-start
  8.0 0.7 compare_select_fusion
  8.6 1.6 %gather_fusion.1 = bf16[128,256]{1,0:T(8,128)(2,1)S(1)} fusion(bf16[128,256]{1,0:T(8,128)(2,1)} %bitcast.103, s32[1024]{0:T(1024)S(1)} %pad_clamp_fusion), kind=kCustom, calls=%fused_computation.2.clone | custom fusion | bytes 131584 | tf_op jit(solution)/shard_map/jit(_take)/gather | solution.py:35
  10.2 1.6 %gather_fusion = bf16[128,256]{1,0:T(8,128)(2,1)S(1)} fusion(bf16[128,256]{1,0:T(8,128)(2,1)} %bitcast.104, s32[1024]{0:T(1024)S(1)} %pad_clamp_fusion), kind=kCustom, calls=%fused_computation.clone | custom fusion | bytes 131584 | tf_op jit(solution)/shard_map/jit(_take)/gather | solution.py:34
  11.9 0.0 copy-start.1
  11.9 0.7 compare_and_fusion
  12.6 0.1 broadcast_select_fusion.5
  12.7 4.0 %collective-permute-start.1 = (bf16[128,512]{1,0:T(8,128)(2,1)S(1)}, bf16[128,512]{1,0:T(8,128)(2,1)S(1)}, u32[]{:S(2)}, u32[]{:S(2)}) collective-permute-start(bf16[128,512]{1,0:T(8,128)(2,1)S(1)} %pad_maximum_fusion.2), channel_id=1, source_target_pairs={{8,0},{16,8},{24,16},{0,24},{9,1},{17,9},{25,17},{1,25},{10,2},{18... | collective-permute-start | bytes 393224 | tf_op jit(solution)/shard_map/ppermute | solution.py:22
  16.7 0.0 collective-permute-start
  16.7 0.0 copy-done.10
  16.7 0.1 copy.29
  16.8 0.1 broadcast_in_dim.65
  16.9 0.1 gt.20
  16.9 0.9 gather_fusion.3
  17.8 0.9 gather_fusion.2
  18.7 0.1 broadcast_select_fusion.1
  18.8 0.2 copy.60
  19.0 0.1 pad_add_fusion
  19.1 1.4 %collective-permute-done.1 = bf16[128,512]{1,0:T(8,128)(2,1)S(1)} collective-permute-done((bf16[128,512]{1,0:T(8,128)(2,1)S(1)}, bf16[128,512]{1,0:T(8,128)(2,1)S(1)}, u32[]{:S(2)}, u32[]{:S(2)}) %collective-permute-start.1) | collective-permute-done | bytes 131104 | tf_op jit(solution)/shard_map/ppermute | solution.py:22
  20.5 2.7 %collective-permute-done = bf16[128,512]{1,0:T(8,128)(2,1)S(1)} collective-permute-done((bf16[128,512]{1,0:T(8,128)(2,1)S(1)}, bf16[128,512]{1,0:T(8,128)(2,1)S(1)}, u32[]{:S(2)}, u32[]{:S(2)}) %collective-permute-start) | collective-permute-done | bytes 131104 | tf_op jit(solution)/shard_map/ppermute | solution.py:19
  23.3 0.2 copy.30
  23.5 0.8 copy.28
  24.3 0.8 fusion.29
  25.1 0.1 fusion.8
  25.2 16.3 %all-gather.2.cloned.1.call-done = bf16[1024,1024]{1,0:T(8,128)(2,1)} async-done(((bf16[128,1024]{1,0:T(8,128)(2,1)}), bf16[1024,1024]{1,0:T(8,128)(2,1)}) %all-gather.2.cloned.1.call-update) | async-done | bytes 2097168 | tf_op jit(solution)/shard_map/all_gather | solution.py:45
  41.5 3.1 %convolution_convert_fusion.1 = bf16[128,1024]{1,0:T(8,128)(2,1)} fusion(bf16[1024,1024]{1,0:T(8,128)(2,1)} %all-gather.2.cloned.1.call-done, bf16[128,1024]{1,0:T(8,128)(2,1)S(1)} %gather_fusion.3, pred[128]{0:T(512)(128)(4,1)S(1)} %compare_and_fusion), kind=kOutput, calls=%fused_computation.19 | convolution fusion | flops 268697600 | bytes 2621568 | tf_op jit(solution)/shard_map/dot_general | solution.py:74
  44.6 1.1 copy.34
  45.8 1.2 multiply_reduce_fusion
  47.0 0.0 copy-start.5
  47.0 0.7 copy-done.5
  47.7 2.1 %convolution_convert_fusion = bf16[1024,1024]{1,0:T(8,128)(2,1)} fusion(bf16[128,1024]{0,1:T(8,128)(2,1)S(1)} %bitcast.107, bf16[128,1024]{1,0:T(8,128)(2,1)S(1)} %gather_fusion.3, pred[128]{0:T(512)(128)(4,1)S(1)} %compare_and_fusion), kind=kOutput, calls=%fused_computation.9 | convolution fusion | flops 269615104 | bytes 2621568 | tf_op jit(solution)/shard_map/dot_general | solution.py:122
  49.8 0.0 reduce-scatter.3.cloned.1.call-update
  49.9 0.0 copy-start.11
  49.9 0.0 copy-start.9
  49.9 0.0 reduce-scatter.5.cloned.1.call-start
  49.9 34.7 %reduce-scatter.3.cloned.1.call-done = bf16[256,1024]{1,0:T(8,128)(2,1)} async-done(((bf16[1024,1024]{1,0:T(8,128)(2,1)}), bf16[256,1024]{1,0:T(8,128)(2,1)}) %reduce-scatter.3.cloned.1.call-update) | async-done | bytes 524304 | tf_op jit(solution)/shard_map/reduce_scatter | solution.py:121
  84.6 2.1 %convert_element_type.71 = f32[256,1024]{1,0:T(8,128)} convert(bf16[256,1024]{1,0:T(8,128)(2,1)} %reduce-scatter.3.cloned.1.call-done) | non-fusion elementwise | flops 262144 | bytes 1572864 | tf_op jit(solution)/shard_map/convert_element_type | solution.py:128
  86.7 0.0 reduce-scatter.5.cloned.1.call-update
  86.8 0.4 fusion.3
  87.2 0.9 copy-done.3
  88.1 1.1 fusion.6
  89.2 1.9 %copy.42 = bf16[384,256]{1,0:T(8,128)(2,1)} copy(bf16[384,256]{0,1:T(8,128)(2,1)} %bitcast.115) | data formatting | bytes 393216 | tf_op jit(solution)/shard_map/reshape | solution.py:104
  91.1 1.1 fusion.7
  92.1 1.1 copy.43
  93.2 1.0 fusion.9
  94.2 1.5 %collective-permute-start.2 = (bf16[128,512]{1,0:T(8,128)(2,1)S(1)}, bf16[128,512]{1,0:T(8,128)(2,1)}, u32[]{:S(2)}, u32[]{:S(2)}) collective-permute-start(bf16[128,512]{1,0:T(8,128)(2,1)S(1)} %get-tuple-element.19), channel_id=1, source_target_pairs={{0,8},{8,16},{16,24},{24,0},{1,9},{9,17},{17,25},{25,1},{2,10},{10... | collective-permute-start | bytes 393224 | tf_op jit(solution)/shard_map/ppermute | solution.py:19
  95.7 1.5 %collective-permute-start.3 = (bf16[128,512]{1,0:T(8,128)(2,1)S(1)}, bf16[128,512]{1,0:T(8,128)(2,1)}, u32[]{:S(2)}, u32[]{:S(2)}) collective-permute-start(bf16[128,512]{1,0:T(8,128)(2,1)S(1)} %get-tuple-element.20), channel_id=1, source_target_pairs={{8,0},{16,8},{24,16},{0,24},{9,1},{17,9},{25,17},{1,25},{10,2},{18... | collective-permute-start | bytes 393224 | tf_op jit(solution)/shard_map/ppermute | solution.py:22
  97.2 2.1 %convolution_convert_fusion.2 = bf16[128,1024]{1,0:T(8,128)(2,1)} fusion(bf16[128,1024]{0,1:T(8,128)(2,1)} %bitcast.108, bf16[1024,1024]{1,0:T(8,128)(2,1)S(1)} %copy-done.2), kind=kOutput, calls=%fused_computation.20 | convolution fusion | flops 268566528 | bytes 2621440 | tf_op jit(solution)/shard_map/dot_general | solution.py:70
  99.3 0.3 fusion.4
  99.6 0.1 copy.38
  99.8 2.2 %scatter_custom_fusion = bf16[128,1024]{1,0:T(8,128)(2,1)} fusion(s32[128]{0:T(128)S(1)} %fusion.21, bf16[128,1024]{1,0:T(8,128)(2,1)} %convolution_convert_fusion.2, bf16[]{:T(256)} %constant.25.clone.1), kind=kCustom, calls=%fused_computation.45 | custom fusion | bytes 262656 | tf_op jit(solution)/shard_map/scatter | solution.py:73
  102.0 1.8 %scatter_custom_fusion.1 = bf16[128,1024]{1,0:T(8,128)(2,1)} fusion(s32[128]{0:T(128)S(1)} %fusion.21, bf16[128,1024]{1,0:T(8,128)(2,1)S(1)} %copy.38, bf16[]{:T(256)} %constant.25.clone.1), kind=kCustom, calls=%fused_computation.43 | custom fusion | bytes 262146 | tf_op jit(solution)/shard_map/scatter | solution.py:93
  103.8 0.0 collective-permute-done.2
  103.8 0.0 collective-permute-done.3
  103.8 1.0 add_convert_fusion
  104.8 1.6 %scatter_custom_fusion.3 = bf16[128,256]{1,0:T(8,128)(2,1)} fusion(s32[128]{0:T(128)S(1)} %fusion.21, bf16[128,512]{1,0:T(8,128)(2,1)S(1)} %add_convert_fusion, bf16[]{:T(256)} %constant.25.clone.1), kind=kCustom, calls=%fused_computation.47 | custom fusion | bytes 131074 | tf_op jit(solution)/shard_map/scatter | solution.py:118
  106.4 1.6 %scatter_custom_fusion.2 = bf16[128,256]{1,0:T(8,128)(2,1)} fusion(s32[128]{0:T(128)S(1)} %fusion.21, bf16[128,512]{1,0:T(8,128)(2,1)S(1)} %add_convert_fusion, bf16[]{:T(256)} %constant.25.clone.1), kind=kCustom, calls=%fused_computation.49 | custom fusion | bytes 131074 | tf_op jit(solution)/shard_map/scatter | solution.py:117
  108.1 11.4 %reduce-scatter.5.cloned.1.call-done = f32[256,128]{1,0:T(8,128)} async-done(((f32[256,1024]{1,0:T(8,128)}), f32[256,128]{1,0:T(8,128)}) %reduce-scatter.5.cloned.1.call-update) | async-done | bytes 131088 | tf_op jit(solution)/shard_map/reduce_scatter | solution.py:129
  119.5 0.9 multiply_bitcast_fusion
  120.4 0.8 copy.44
  (25 shorter events, 0.1 us)
Async XLA Ops:
  7.2 9.8 %copy-start = (bf16[1,128,1024]{2,1,0:T(8,128)(2,1)S(1)}, bf16[1,128,1024]{2,1,0:T(8,128)(2,1)}, u32[]{:S(2)}) copy-start(bf16[1,128,1024]{2,1,0:T(8,128)(2,1)} %param.17) | copy-start | bytes 786436
  7.2 9.5 %copy-start.10 = (s32[1,4,8]{2,1,0:T(4,128)S(1)}, s32[1,4,8]{2,1,0:T(4,128)}, u32[]{:S(2)}) copy-start(s32[1,4,8]{2,1,0:T(4,128)} %param.15) | copy-start | bytes 388
  7.2 34.3 %all-gather.2.cloned.1.call-start = ((), (), s32[]{:S(2)}) async-start(), calls=%async_computation.2 | async-start | bytes 2359296 | tf_op jit(solution)/shard_map/all_gather | solution.py:45
  7.9 76.7 %reduce-scatter.3.cloned.1.call-start = ((), (), s32[]{:S(2)}) async-start(), calls=%async_computation.3 | async-start | bytes 2621440 | tf_op jit(solution)/shard_map/reduce_scatter | solution.py:121
  11.9 6.0 %copy-start.1 = (bf16[1,128,1024]{2,1,0:T(8,128)(2,1)S(1)}, bf16[1,128,1024]{2,1,0:T(8,128)(2,1)}, u32[]{:S(2)}) copy-start(bf16[1,128,1024]{2,1,0:T(8,128)(2,1)} %param.11) | copy-start | bytes 786436
  12.7 7.9 %collective-permute-start.1 = (bf16[128,512]{1,0:T(8,128)(2,1)S(1)}, bf16[128,512]{1,0:T(8,128)(2,1)S(1)}, u32[]{:S(2)}, u32[]{:S(2)}) collective-permute-start(bf16[128,512]{1,0:T(8,128)(2,1)S(1)} %pad_maximum_fusion.2), channel_id=1, source_target_pairs={{8,0},{16,8},{24,16},{0,24},{9,1},{17,9},{25,17},{1,25},{10,2},{18... | collective-permute-start | bytes 393224 | tf_op jit(solution)/shard_map/ppermute | solution.py:22
  16.7 6.6 %collective-permute-start = (bf16[128,512]{1,0:T(8,128)(2,1)S(1)}, bf16[128,512]{1,0:T(8,128)(2,1)S(1)}, u32[]{:S(2)}, u32[]{:S(2)}) collective-permute-start(bf16[128,512]{1,0:T(8,128)(2,1)S(1)} %pad_maximum_fusion.2), channel_id=1, source_target_pairs={{0,8},{8,16},{16,24},{24,0},{1,9},{9,17},{17,25},{25,1},{2,10},{10... | collective-permute-start | bytes 393224 | tf_op jit(solution)/shard_map/ppermute | solution.py:19
  23.4 1.6 %copy-start.7 = (bf16[384,256]{0,1:T(8,128)(2,1)}, bf16[384,256]{0,1:T(8,128)(2,1)S(1)}, u32[]{:S(2)}) copy-start(bf16[384,256]{0,1:T(8,128)(2,1)S(1)} %copy.30) | copy-start | bytes 589828
  47.0 0.7 copy-start.5
  49.9 36.9 %copy-start.11 = (s32[1,1,128]{2,1,0:T(1,128)S(1)}, s32[1,1,128]{2,1,0:T(1,128)}, u32[]{:S(2)}) copy-start(s32[1,1,128]{2,1,0:T(1,128)} %param.14) | copy-start | bytes 1540
  49.9 36.9 %copy-start.9 = (bf16[384,256]{0,1:T(8,128)(2,1)S(1)}, bf16[384,256]{0,1:T(8,128)(2,1)}, u32[]{:S(2)}) copy-start(bf16[384,256]{0,1:T(8,128)(2,1)} %copy.28) | copy-start | bytes 589828
  49.9 69.6 %reduce-scatter.5.cloned.1.call-start = ((), (), s32[]{:S(2)}) async-start(), calls=%async_computation.4 | async-start | bytes 1179648 | tf_op jit(solution)/shard_map/reduce_scatter | solution.py:129
  87.2 0.9 copy-start.3
  89.2 8.0 %copy-start.2 = (bf16[1024,1024]{1,0:T(8,128)(2,1)S(1)}, bf16[1024,1024]{1,0:T(8,128)(2,1)}, u32[]{:S(2)}) copy-start(bf16[1024,1024]{1,0:T(8,128)(2,1)} %all-gather.2.cloned.1.call-done) | copy-start | bytes 6291460
  93.2 6.1 %copy-start.4 = (bf16[2,4,128,384]{2,3,1,0:T(8,128)(2,1)S(1)}, bf16[2,4,128,384]{2,3,1,0:T(8,128)(2,1)}, u32[]{:S(2)}) copy-start(bf16[2,4,128,384]{2,3,1,0:T(8,128)(2,1)} %copy-done.3) | copy-start | bytes 2359300
  93.2 6.1 %copy-start.8 = (bf16[384,256]{0,1:T(8,128)(2,1)S(1)}, bf16[384,256]{0,1:T(8,128)(2,1)}, u32[]{:S(2)}) copy-start(bf16[384,256]{0,1:T(8,128)(2,1)} %copy-done.7) | copy-start | bytes 589828
  94.2 9.6 %collective-permute-start.2 = (bf16[128,512]{1,0:T(8,128)(2,1)S(1)}, bf16[128,512]{1,0:T(8,128)(2,1)}, u32[]{:S(2)}, u32[]{:S(2)}) collective-permute-start(bf16[128,512]{1,0:T(8,128)(2,1)S(1)} %get-tuple-element.19), channel_id=1, source_target_pairs={{0,8},{8,16},{16,24},{24,0},{1,9},{9,17},{17,25},{25,1},{2,10},{10... | collective-permute-start | bytes 393224 | tf_op jit(solution)/shard_map/ppermute | solution.py:19
  95.7 8.1 %collective-permute-start.3 = (bf16[128,512]{1,0:T(8,128)(2,1)S(1)}, bf16[128,512]{1,0:T(8,128)(2,1)}, u32[]{:S(2)}, u32[]{:S(2)}) collective-permute-start(bf16[128,512]{1,0:T(8,128)(2,1)S(1)} %get-tuple-element.20), channel_id=1, source_target_pairs={{8,0},{16,8},{24,16},{0,24},{9,1},{17,9},{25,17},{1,25},{10,2},{18... | collective-permute-start | bytes 393224 | tf_op jit(solution)/shard_map/ppermute | solution.py:22
  99.3 4.5 %copy-start.6 = (bf16[384,256]{1,0:T(8,128)(2,1)S(1)}, bf16[384,256]{1,0:T(8,128)(2,1)}, u32[]{:S(2)}) copy-start(bf16[384,256]{1,0:T(8,128)(2,1)} %copy.42) | copy-start | bytes 589828
Sparse Core Ops, SparseCore 0:
  9.6 31.8 all-gather.1
  50.0 34.5 reduce-scatter.2
  86.9 32.5 reduce-scatter.4
where the time goes:
time: 128 us
  waiting for transfers between devices  67.2 us (52%)
  local copies, waits for them, and re-layouts  20.3 us (16%)
  between operations  14 us (11%)
  matrix products  12.3 us (10%)
  starting transfers between devices  7.07 us (6%)
  other arithmetic  6.9 us (5%)
    reduce_scatter x1, waiting for transfers between devices, shards(): lax.psum_scatter(lax.dot_general(dy_seq, attended, (((0,), (0,)), ((), ()...  34.7 us
    all_gather x1, waiting for transfers between devices, shards(): weight_all = lax.all_gather(out_weight, 'dp', axis=0, tiled=True)  16.3 us
    reduce_scatter x1, waiting for transfers between devices, shards(): lax.psum_scatter(tile_rows, 'dp', scatter_dimension=1, tiled=True)  11.4 us
    ppermute x2, starting transfers between devices, with_halo(): lax.ppermute(lax.slice_in_dim(block, 0, width, axis=dim), axis, backward)  5.44 us
    dot_general x1, matrix products, shards(): lax.dot_general(dy_seq, weight_all, (((1,), (1,)), ((), ())), preferred_e...  3.13 us
    ppermute x2, waiting for transfers between devices, with_halo(): lax.ppermute(lax.slice_in_dim(block, block.shape[dim] - width, None, axis...  2.67 us
  transfers between devices with their start and end apart: 7, of which 5 were waited for; matrix products, arithmetic and copies ran while one was open for 21% of the time, Pallas kernels for 0%

commit v1 on v0

--- a/solution.py
+++ b/solution.py
@@ -42,7 +42,12 @@
     value_band = neighbour_band[:, key_head_width:].reshape(
         3 * token_rows, KEY_VALUE_HEADS, HEAD_WIDTH
     )
-    weight_all = lax.all_gather(out_weight, "dp", axis=0, tiled=True)
+    ring = [out_weight]
+    for hop in range(7):
+        ring.append(lax.ppermute(ring[-1], "dp", [(dev, (dev + 1) % 8) for dev in range(8)]))
+    weight_all = jnp.roll(
+        jnp.concatenate(ring[::-1], axis=0), (lax.axis_index("dp") + 1) * ring[0].shape[0], axis=0
+    )
     expanded = jnp.repeat(jnp.repeat(block_mask[0], BLK, 0), BLK, 1) > 0
     allowed = jnp.concatenate(
         [

time: 128 us -> 152 us (1.19)
  waiting for transfers between devices: 67.2 us -> 93.9 us
  matrix products: 12.3 us -> 10.1 us
    ppermute x0 -> x7, waiting for transfers between devices: none -> 41.5 us  [shards(): lax.ppermute(ring[-1], 'dp', [(dev, (dev + 1) % 8) for dev in range(8)])]
    all_gather x1 -> x0, waiting for transfers between devices: 16.3 us -> none  [shards(): weight_all = lax.all_gather(out_weight, 'dp', axis=0, tiled=True)]
    reduce_scatter x1, waiting for transfers between devices: 11.4 us -> 17.3 us  [shards(): lax.psum_scatter(tile_rows, 'dp', scatter_dimension=1, tiled=True)]
    unnamed x25 -> x50, local copies, waits for them, and re-layouts: 2.39 us -> 7.83 us
    dot_general x1, matrix products: 3.13 us -> 0.84 us  [shards(): lax.dot_general(dy_seq, weight_all, (((1,), (1,)), ((), ())), preferred_e...]
    reshape x1, local copies, waits for them, and re-layouts: 1.89 us -> 0.15 us  [shards(): part_k.reshape(3 * token_rows, key_head_width)]
    ppermute x2, waiting for transfers between devices: 2.67 us -> 1.06 us  [with_halo(): lax.ppermute(lax.slice_in_dim(block, block.shape[dim] - width, None, axis...]
  transfers between devices with their start and end apart: 7 -> 13, of which waited for: 5 -> 10; matrix products, arithmetic and copies ran while one was open for 21% -> 15% of each run, Pallas kernels for 0% -> 0%
where the time goes in v1:
time: 152 us
  waiting for transfers between devices  93.9 us (62%)
  local copies, waits for them, and re-layouts  21.7 us (14%)
  between operations  14.6 us (10%)
  matrix products  10.1 us (7%)
  starting transfers between devices  5.71 us (4%)
  other arithmetic  5.61 us (4%)
    ppermute x7, waiting for transfers between devices, shards(): lax.ppermute(ring[-1], 'dp', [(dev, (dev + 1) % 8) for dev in range(8)])  41.5 us
    reduce_scatter x1, waiting for transfers between devices, shards(): lax.psum_scatter(lax.dot_general(dy_seq, attended, (((0,), (0,)), ((), ()...  34 us
    reduce_scatter x1, waiting for transfers between devices, shards(): lax.psum_scatter(tile_rows, 'dp', scatter_dimension=1, tiled=True)  17.3 us
    unnamed x50, local copies, waits for them, and re-layouts  7.83 us
    ppermute x2, starting transfers between devices, with_halo(): lax.ppermute(lax.slice_in_dim(block, 0, width, axis=dim), axis, backward)  4.51 us
  transfers between devices with their start and end apart: 13, of which 10 were waited for; matrix products, arithmetic and copies ran while one was open for 15% of the time, Pallas kernels for 0%

profile of v1, /device:TPU:0, one launch (start us, length us, event | category | flops | bytes accessed | tf_op | source)
XLA Modules:
  0.0 151.6 jit_solution(1807341030441460061)
XLA Ops:
  7.2 0.0 copy-start
  7.2 0.0 reduce-scatter.3.cloned.1.call-start
  7.2 0.5 collective-permute-start.2
  7.8 0.7 compare_select_fusion
  8.4 1.6 %gather_fusion = bf16[128,256]{1,0:T(8,128)(2,1)S(1)} fusion(bf16[128,256]{1,0:T(8,128)(2,1)} %bitcast.97, s32[1024]{0:T(1024)S(1)} %pad_clamp_fusion), kind=kCustom, calls=%fused_computation.clone | custom fusion | bytes 131584 | tf_op jit(solution)/shard_map/jit(_take)/gather | solution.py:34
  10.1 1.6 %gather_fusion.1 = bf16[128,256]{1,0:T(8,128)(2,1)S(1)} fusion(bf16[128,256]{1,0:T(8,128)(2,1)} %bitcast.98, s32[1024]{0:T(1024)S(1)} %pad_clamp_fusion), kind=kCustom, calls=%fused_computation.2.clone | custom fusion | bytes 131584 | tf_op jit(solution)/shard_map/jit(_take)/gather | solution.py:35
  11.7 0.7 compare_and_fusion
  12.3 3.8 %collective-permute-done.2 = bf16[128,1024]{1,0:T(8,128)(2,1)S(1)} collective-permute-done((bf16[128,1024]{1,0:T(8,128)(2,1)}, bf16[128,1024]{1,0:T(8,128)(2,1)S(1)}, u32[]{:S(2)}, u32[]{:S(2)}) %collective-permute-start.2) | collective-permute-done | bytes 262176 | tf_op jit(solution)/shard_map/ppermute | solution.py:47
  16.1 0.1 broadcast_select_fusion.5
  16.2 3.0 %collective-permute-start.1 = (bf16[128,512]{1,0:T(8,128)(2,1)S(1)}, bf16[128,512]{1,0:T(8,128)(2,1)S(1)}, u32[]{:S(2)}, u32[]{:S(2)}) collective-permute-start(bf16[128,512]{1,0:T(8,128)(2,1)S(1)} %pad_maximum_fusion.2), channel_id=1, source_target_pairs={{8,0},{16,8},{24,16},{0,24},{9,1},{17,9},{25,17},{1,25},{10,2},{18... | collective-permute-start | bytes 393224 | tf_op jit(solution)/shard_map/ppermute | solution.py:22
  19.2 4.5 %collective-permute-done.3 = bf16[128,1024]{1,0:T(8,128)(2,1)S(1)} collective-permute-done((bf16[128,1024]{1,0:T(8,128)(2,1)S(1)}, bf16[128,1024]{1,0:T(8,128)(2,1)S(1)}, u32[]{:S(2)}, u32[]{:S(2)}) %collective-permute-start.3) | collective-permute-done | bytes 262176 | tf_op jit(solution)/shard_map/ppermute | solution.py:47
  23.7 0.7 compare_bitcast_fusion
  24.4 0.9 gather_fusion.2
  25.2 0.1 copy.29
  25.3 0.1 broadcast_in_dim.65
  25.4 0.1 gt.20
  25.5 0.1 broadcast_select_fusion.1
  25.6 5.7 %collective-permute-done.4 = bf16[128,1024]{1,0:T(8,128)(2,1)S(1)} collective-permute-done((bf16[128,1024]{1,0:T(8,128)(2,1)S(1)}, bf16[128,1024]{1,0:T(8,128)(2,1)S(1)}, u32[]{:S(2)}, u32[]{:S(2)}) %collective-permute-start.4) | collective-permute-done | bytes 262176 | tf_op jit(solution)/shard_map/ppermute | solution.py:47
  31.3 0.9 gather_fusion.3
  32.2 0.2 copy.60
  32.4 0.1 pad_add_fusion
  32.5 6.3 %collective-permute-done.5 = bf16[128,1024]{1,0:T(8,128)(2,1)S(1)} collective-permute-done((bf16[128,1024]{1,0:T(8,128)(2,1)S(1)}, bf16[128,1024]{1,0:T(8,128)(2,1)S(1)}, u32[]{:S(2)}, u32[]{:S(2)}) %collective-permute-start.5) | collective-permute-done | bytes 262176 | tf_op jit(solution)/shard_map/ppermute | solution.py:47
  39.0 0.8 copy.28
  39.8 0.2 copy.30
  40.0 6.6 %collective-permute-done.6 = bf16[128,1024]{1,0:T(8,128)(2,1)} collective-permute-done((bf16[128,1024]{1,0:T(8,128)(2,1)S(1)}, bf16[128,1024]{1,0:T(8,128)(2,1)}, u32[]{:S(2)}, u32[]{:S(2)}) %collective-permute-start.6) | collective-permute-done | bytes 262176 | tf_op jit(solution)/shard_map/ppermute | solution.py:47
  46.6 0.0 copy-start.4
  46.6 0.8 fusion.41
  47.5 7.0 %collective-permute-done.7 = bf16[128,1024]{1,0:T(8,128)(2,1)} collective-permute-done((bf16[128,1024]{1,0:T(8,128)(2,1)}, bf16[128,1024]{1,0:T(8,128)(2,1)}, u32[]{:S(2)}, u32[]{:S(2)}) %collective-permute-start.7) | collective-permute-done | bytes 262176 | tf_op jit(solution)/shard_map/ppermute | solution.py:47
  54.5 0.1 fusion.18
  54.6 7.7 %collective-permute-done.8 = bf16[128,1024]{1,0:T(8,128)(2,1)S(1)} collective-permute-done((bf16[128,1024]{1,0:T(8,128)(2,1)}, bf16[128,1024]{1,0:T(8,128)(2,1)S(1)}, u32[]{:S(2)}, u32[]{:S(2)}) %collective-permute-start.8) | collective-permute-done | bytes 262176 | tf_op jit(solution)/shard_map/ppermute | solution.py:47
  62.3 1.0 constant_dynamic-update-slice_fusion.14
  63.3 1.0 constant_dynamic-update-slice_fusion.13
  64.3 1.0 constant_dynamic-update-slice_fusion.12
  65.4 1.0 constant_dynamic-update-slice_fusion.6
  66.4 1.0 constant_dynamic-update-slice_fusion.5
  67.5 2.0 %copy-done.2 = bf16[2048,1024]{1,0:T(8,128)(2,1)} copy-done((bf16[2048,1024]{1,0:T(8,128)(2,1)}, bf16[2048,1024]{1,0:T(8,128)(2,1)S(1)}, u32[]{:S(2)}) %copy-start.2) | copy-done | bytes 4194328
  69.5 0.8 fusion.12
  70.3 0.2 copy.34
  70.5 1.3 multiply_reduce_fusion
  71.8 2.2 %convolution_convert_fusion = bf16[1024,1024]{1,0:T(8,128)(2,1)} fusion(bf16[128,1024]{0,1:T(8,128)(2,1)S(1)} %bitcast.101, bf16[128,1024]{1,0:T(8,128)(2,1)S(1)} %gather_fusion.3, pred[128]{0:T(512)(128)(4,1)S(1)} %compare_and_fusion), kind=kOutput, calls=%fused_computation.9 | convolution fusion | flops 269615104 | bytes 2621568 | tf_op jit(solution)/shard_map/dot_general | solution.py:127
  74.0 0.0 reduce-scatter.3.cloned.1.call-update
  74.0 0.0 reduce-scatter.5.cloned.1.call-start
  74.1 34.0 %reduce-scatter.3.cloned.1.call-done = bf16[256,1024]{1,0:T(8,128)(2,1)} async-done(((bf16[1024,1024]{1,0:T(8,128)(2,1)}), bf16[256,1024]{1,0:T(8,128)(2,1)}) %reduce-scatter.3.cloned.1.call-update) | async-done | bytes 524304 | tf_op jit(solution)/shard_map/reduce_scatter | solution.py:126
  108.1 2.1 %convert_element_type.71 = f32[256,1024]{1,0:T(8,128)} convert(bf16[256,1024]{1,0:T(8,128)(2,1)} %reduce-scatter.3.cloned.1.call-done) | non-fusion elementwise | flops 262144 | bytes 1572864 | tf_op jit(solution)/shard_map/convert_element_type | solution.py:133
  110.2 0.0 reduce-scatter.5.cloned.1.call-update
  110.3 1.8 %fusion.7 = bf16[2,4,128,384]{2,3,1,0:T(8,128)(2,1)S(1)} fusion(bf16[384,2,128,1]{0,2,3,1:T(8,128)(2,1)S(1)} %bitcast.111, bf16[128,2,4,128]{0,3,2,1:T(8,128)(2,1)S(1)} %bitcast.99, f32[2,4,128]{2,1,0:T(4,128)S(1)} %bitcast.117, f32[2,4,128,384]{2,3,1,0:T(8,128)} %copy-done.3, f32[2,4,128]{2,1,0:T(4,128)S(1)} %get-tuple-element.27), kind=kOutput, calls=%fused_computation.17 | convolution fusion | flops 102236160 | bytes 2826240 | tf_op jit(solution)/shard_map/tkgd,skd->kgts/dot_general | solution.py:85
  112.1 0.3 fusion.8
  112.4 0.1 copy.38
  112.6 0.4 fusion.16
  113.0 0.1 copy.42
  113.1 0.4 fusion.17
  113.5 0.1 copy.43
  113.7 1.5 collective-permute-start.10
  115.2 0.6 collective-permute-start.9
  115.7 2.1 %fusion.9 = bf16[128,1024]{1,0:T(8,128)(2,1)S(1)} fusion(bf16[128,1024]{0,1:T(8,128)(2,1)S(1)} %bitcast.102, bf16[2048,1024]{1,0:T(8,128)(2,1)} %copy-done.2, s32[]{:T(128)S(6)} %select_n.50), kind=kOutput, calls=%fused_computation.23 | convolution fusion | flops 268566528 | bytes 2621444 | tf_op jit(solution)/shard_map/dot_general | solution.py:75
  117.8 1.8 %scatter_custom_fusion = bf16[128,1024]{1,0:T(8,128)(2,1)} fusion(s32[128]{0:T(128)S(1)} %fusion.31, bf16[128,1024]{1,0:T(8,128)(2,1)S(1)} %fusion.9, bf16[]{:T(256)} %constant.30.clone.1), kind=kCustom, calls=%fused_computation.49 | custom fusion | bytes 262146 | tf_op jit(solution)/shard_map/scatter | solution.py:78
  119.6 1.8 %scatter_custom_fusion.1 = bf16[128,1024]{1,0:T(8,128)(2,1)} fusion(s32[128]{0:T(128)S(1)} %fusion.31, bf16[128,1024]{1,0:T(8,128)(2,1)S(1)} %copy.38, bf16[]{:T(256)} %constant.30.clone.1), kind=kCustom, calls=%fused_computation.47 | custom fusion | bytes 262146 | tf_op jit(solution)/shard_map/scatter | solution.py:98
  121.4 1.1 collective-permute-done.9
  122.5 0.1 add_convert_fusion
  122.6 1.6 %scatter_custom_fusion.2 = bf16[128,256]{1,0:T(8,128)(2,1)} fusion(s32[128]{0:T(128)S(1)} %fusion.31, bf16[128,512]{1,0:T(8,128)(2,1)S(1)} %add_convert_fusion, bf16[]{:T(256)} %constant.30.clone.1), kind=kCustom, calls=%fused_computation.53 | custom fusion | bytes 131074 | tf_op jit(solution)/shard_map/scatter | solution.py:122
  124.2 1.6 %scatter_custom_fusion.3 = bf16[128,256]{1,0:T(8,128)(2,1)} fusion(s32[128]{0:T(128)S(1)} %fusion.31, bf16[128,512]{1,0:T(8,128)(2,1)S(1)} %add_convert_fusion, bf16[]{:T(256)} %constant.30.clone.1), kind=kCustom, calls=%fused_computation.51 | custom fusion | bytes 131074 | tf_op jit(solution)/shard_map/scatter | solution.py:123
  125.8 17.3 %reduce-scatter.5.cloned.1.call-done = f32[256,128]{1,0:T(8,128)} async-done(((f32[256,1024]{1,0:T(8,128)}), f32[256,128]{1,0:T(8,128)}) %reduce-scatter.5.cloned.1.call-update) | async-done | bytes 131088 | tf_op jit(solution)/shard_map/reduce_scatter | solution.py:134
  143.1 0.9 multiply_bitcast_fusion
  144.0 0.8 copy.44
  (62 shorter events, 0.4 us)
Async XLA Ops:
  7.2 17.2 %copy-start = (bf16[1,128,1024]{2,1,0:T(8,128)(2,1)S(1)}, bf16[1,128,1024]{2,1,0:T(8,128)(2,1)}, u32[]{:S(2)}) copy-start(bf16[1,128,1024]{2,1,0:T(8,128)(2,1)} %param.11) | copy-start | bytes 786436
  7.2 24.2 %copy-start.1 = (bf16[1,128,1024]{2,1,0:T(8,128)(2,1)S(1)}, bf16[1,128,1024]{2,1,0:T(8,128)(2,1)}, u32[]{:S(2)}) copy-start(bf16[1,128,1024]{2,1,0:T(8,128)(2,1)} %param.17) | copy-start | bytes 786436
  7.2 100.9 %reduce-scatter.3.cloned.1.call-start = ((), (), s32[]{:S(2)}) async-start(), calls=%async_computation.2 | async-start | bytes 2621440 | tf_op jit(solution)/shard_map/reduce_scatter | solution.py:126
  7.2 8.8 %collective-permute-start.2 = (bf16[128,1024]{1,0:T(8,128)(2,1)}, bf16[128,1024]{1,0:T(8,128)(2,1)S(1)}, u32[]{:S(2)}, u32[]{:S(2)}) collective-permute-start(bf16[128,1024]{1,0:T(8,128)(2,1)} %param.16), channel_id=1, source_target_pairs={{0,1},{1,2},{2,3},{3,4},{4,5},{5,6},{6,7},{7,0},{8,9},{9,10},{10,1... | collective-permute-start | bytes 786440 | tf_op jit(solution)/shard_map/ppermute | solution.py:47
  16.1 8.3 %copy-start.5 = (bf16[128,1024]{1,0:T(8,128)(2,1)}, bf16[128,1024]{1,0:T(8,128)(2,1)S(1)}, u32[]{:S(2)}) copy-start(bf16[128,1024]{1,0:T(8,128)(2,1)S(1)} %collective-permute-done.2) | copy-start | bytes 786436
  16.1 7.6 %collective-permute-start.3 = (bf16[128,1024]{1,0:T(8,128)(2,1)S(1)}, bf16[128,1024]{1,0:T(8,128)(2,1)S(1)}, u32[]{:S(2)}, u32[]{:S(2)}) collective-permute-start(bf16[128,1024]{1,0:T(8,128)(2,1)S(1)} %collective-permute-done.2), channel_id=1, source_target_pairs={{0,1},{1,2},{2,3},{3,4},{4,5},{5,6},{6,7},{7,0},{8,9},{9,10},{10,1... | collective-permute-start | bytes 786440 | tf_op jit(solution)/shard_map/ppermute | solution.py:47
  16.2 22.7 %collective-permute-start.1 = (bf16[128,512]{1,0:T(8,128)(2,1)S(1)}, bf16[128,512]{1,0:T(8,128)(2,1)S(1)}, u32[]{:S(2)}, u32[]{:S(2)}) collective-permute-start(bf16[128,512]{1,0:T(8,128)(2,1)S(1)} %pad_maximum_fusion.2), channel_id=1, source_target_pairs={{8,0},{16,8},{24,16},{0,24},{9,1},{17,9},{25,17},{1,25},{10,2},{18... | collective-permute-start | bytes 393224 | tf_op jit(solution)/shard_map/ppermute | solution.py:22
  19.2 19.7 %collective-permute-start = (bf16[128,512]{1,0:T(8,128)(2,1)S(1)}, bf16[128,512]{1,0:T(8,128)(2,1)S(1)}, u32[]{:S(2)}, u32[]{:S(2)}) collective-permute-start(bf16[128,512]{1,0:T(8,128)(2,1)S(1)} %pad_maximum_fusion.2), channel_id=1, source_target_pairs={{0,8},{8,16},{16,24},{24,0},{1,9},{9,17},{17,25},{25,1},{2,10},{10... | collective-permute-start | bytes 393224 | tf_op jit(solution)/shard_map/ppermute | solution.py:19
  23.7 7.7 %copy-start.7 = (bf16[128,1024]{1,0:T(8,128)(2,1)}, bf16[128,1024]{1,0:T(8,128)(2,1)S(1)}, u32[]{:S(2)}) copy-start(bf16[128,1024]{1,0:T(8,128)(2,1)S(1)} %collective-permute-done.3) | copy-start | bytes 786436
  23.7 7.6 %collective-permute-start.4 = (bf16[128,1024]{1,0:T(8,128)(2,1)S(1)}, bf16[128,1024]{1,0:T(8,128)(2,1)S(1)}, u32[]{:S(2)}, u32[]{:S(2)}) collective-permute-start(bf16[128,1024]{1,0:T(8,128)(2,1)S(1)} %collective-permute-done.3), channel_id=1, source_target_pairs={{0,1},{1,2},{2,3},{3,4},{4,5},{5,6},{6,7},{7,0},{8,9},{9,10},{10,1... | collective-permute-start | bytes 786440 | tf_op jit(solution)/shard_map/ppermute | solution.py:47
  31.3 15.3 %copy-start.9 = (bf16[128,1024]{1,0:T(8,128)(2,1)}, bf16[128,1024]{1,0:T(8,128)(2,1)S(1)}, u32[]{:S(2)}) copy-start(bf16[128,1024]{1,0:T(8,128)(2,1)S(1)} %collective-permute-done.4) | copy-start | bytes 786436
  31.3 7.6 %collective-permute-start.5 = (bf16[128,1024]{1,0:T(8,128)(2,1)S(1)}, bf16[128,1024]{1,0:T(8,128)(2,1)S(1)}, u32[]{:S(2)}, u32[]{:S(2)}) collective-permute-start(bf16[128,1024]{1,0:T(8,128)(2,1)S(1)} %collective-permute-done.4), channel_id=1, source_target_pairs={{0,1},{1,2},{2,3},{3,4},{4,5},{5,6},{6,7},{7,0},{8,9},{9,10},{10,1... | collective-permute-start | bytes 786440 | tf_op jit(solution)/shard_map/ppermute | solution.py:47
  38.9 7.7 %copy-start.11 = (bf16[128,1024]{1,0:T(8,128)(2,1)}, bf16[128,1024]{1,0:T(8,128)(2,1)S(1)}, u32[]{:S(2)}) copy-start(bf16[128,1024]{1,0:T(8,128)(2,1)S(1)} %collective-permute-done.5) | copy-start | bytes 786436
  38.9 7.7 %collective-permute-start.6 = (bf16[128,1024]{1,0:T(8,128)(2,1)S(1)}, bf16[128,1024]{1,0:T(8,128)(2,1)}, u32[]{:S(2)}, u32[]{:S(2)}) collective-permute-start(bf16[128,1024]{1,0:T(8,128)(2,1)S(1)} %collective-permute-done.5), channel_id=1, source_target_pairs={{0,1},{1,2},{2,3},{3,4},{4,5},{5,6},{6,7},{7,0},{8,9},{9,10},{10,1... | collective-permute-start | bytes 786440 | tf_op jit(solution)/shard_map/ppermute | solution.py:47
  40.0 14.5 %copy-start.13 = (bf16[384,256]{0,1:T(8,128)(2,1)}, bf16[384,256]{0,1:T(8,128)(2,1)S(1)}, u32[]{:S(2)}) copy-start(bf16[384,256]{0,1:T(8,128)(2,1)S(1)} %copy.30) | copy-start | bytes 589828
  46.6 7.9 %collective-permute-start.7 = (bf16[128,1024]{1,0:T(8,128)(2,1)}, bf16[128,1024]{1,0:T(8,128)(2,1)}, u32[]{:S(2)}, u32[]{:S(2)}) collective-permute-start(bf16[128,1024]{1,0:T(8,128)(2,1)} %collective-permute-done.6), channel_id=1, source_target_pairs={{0,1},{1,2},{2,3},{3,4},{4,5},{5,6},{6,7},{7,0},{8,9},{9,10},{10,1... | collective-permute-start | bytes 786440 | tf_op jit(solution)/shard_map/ppermute | solution.py:47
  46.6 18.8 %copy-start.4 = (bf16[128,1024]{1,0:T(8,128)(2,1)S(1)}, bf16[128,1024]{1,0:T(8,128)(2,1)}, u32[]{:S(2)}) copy-start(bf16[128,1024]{1,0:T(8,128)(2,1)} %param.16) | copy-start | bytes 786436
  47.4 20.0 %copy-start.3 = (f32[2,4,128,384]{2,3,1,0:T(8,128)}, f32[2,4,128,384]{2,3,1,0:T(8,128)S(1)}, u32[]{:S(2)}) copy-start(f32[2,4,128,384]{2,3,1,0:T(8,128)S(1)} %get-tuple-element.28) | copy-start | bytes 4718596
  47.4 17.8 %copy-start.10 = (bf16[128,1024]{1,0:T(8,128)(2,1)S(1)}, bf16[128,1024]{1,0:T(8,128)(2,1)}, u32[]{:S(2)}) copy-start(bf16[128,1024]{1,0:T(8,128)(2,1)} %copy-done.9) | copy-start | bytes 786436
  47.4 17.8 %copy-start.8 = (bf16[128,1024]{1,0:T(8,128)(2,1)S(1)}, bf16[128,1024]{1,0:T(8,128)(2,1)}, u32[]{:S(2)}) copy-start(bf16[128,1024]{1,0:T(8,128)(2,1)} %copy-done.7) | copy-start | bytes 786436
  47.4 17.9 %copy-start.6 = (bf16[128,1024]{1,0:T(8,128)(2,1)S(1)}, bf16[128,1024]{1,0:T(8,128)(2,1)}, u32[]{:S(2)}) copy-start(bf16[128,1024]{1,0:T(8,128)(2,1)} %copy-done.5) | copy-start | bytes 786436
  47.4 19.9 %copy-start.12 = (bf16[128,1024]{1,0:T(8,128)(2,1)S(1)}, bf16[128,1024]{1,0:T(8,128)(2,1)}, u32[]{:S(2)}) copy-start(bf16[128,1024]{1,0:T(8,128)(2,1)} %copy-done.11) | copy-start | bytes 786436
  54.5 7.8 %collective-permute-start.8 = (bf16[128,1024]{1,0:T(8,128)(2,1)}, bf16[128,1024]{1,0:T(8,128)(2,1)S(1)}, u32[]{:S(2)}, u32[]{:S(2)}) collective-permute-start(bf16[128,1024]{1,0:T(8,128)(2,1)} %collective-permute-done.7), channel_id=1, source_target_pairs={{0,1},{1,2},{2,3},{3,4},{4,5},{5,6},{6,7},{7,0},{8,9},{9,10},{10,1... | collective-permute-start | bytes 786440 | tf_op jit(solution)/shard_map/ppermute | solution.py:47
  67.5 2.0 %copy-start.2 = (bf16[2048,1024]{1,0:T(8,128)(2,1)}, bf16[2048,1024]{1,0:T(8,128)(2,1)S(1)}, u32[]{:S(2)}) copy-start(bf16[2048,1024]{1,0:T(8,128)(2,1)S(1)} %constant_dynamic-update-slice_fusion) | copy-start | bytes 12582916
  70.5 39.7 %copy-start.16 = (s32[1,1,128]{2,1,0:T(1,128)S(1)}, s32[1,1,128]{2,1,0:T(1,128)}, u32[]{:S(2)}) copy-start(s32[1,1,128]{2,1,0:T(1,128)} %param.14) | copy-start | bytes 1540
  70.5 39.7 %copy-start.15 = (bf16[384,256]{0,1:T(8,128)(2,1)S(1)}, bf16[384,256]{0,1:T(8,128)(2,1)}, u32[]{:S(2)}) copy-start(bf16[384,256]{0,1:T(8,128)(2,1)} %copy.28) | copy-start | bytes 589828
  74.0 38.1 %copy-start.14 = (bf16[384,256]{0,1:T(8,128)(2,1)S(1)}, bf16[384,256]{0,1:T(8,128)(2,1)}, u32[]{:S(2)}) copy-start(bf16[384,256]{0,1:T(8,128)(2,1)} %copy-done.13) | copy-start | bytes 589828
  74.0 69.1 %reduce-scatter.5.cloned.1.call-start = ((), (), s32[]{:S(2)}) async-start(), calls=%async_computation.3 | async-start | bytes 1179648 | tf_op jit(solution)/shard_map/reduce_scatter | solution.py:134
  113.7 7.8 %collective-permute-start.10 = (bf16[128,512]{1,0:T(8,128)(2,1)S(1)}, bf16[128,512]{1,0:T(8,128)(2,1)S(1)}, u32[]{:S(2)}, u32[]{:S(2)}) collective-permute-start(bf16[128,512]{1,0:T(8,128)(2,1)S(1)} %get-tuple-element.20), channel_id=1, source_target_pairs={{8,0},{16,8},{24,16},{0,24},{9,1},{17,9},{25,17},{1,25},{10,2},{18... | collective-permute-start | bytes 393224 | tf_op jit(solution)/shard_map/ppermute | solution.py:22
  115.2 7.3 %collective-permute-start.9 = (bf16[128,512]{1,0:T(8,128)(2,1)S(1)}, bf16[128,512]{1,0:T(8,128)(2,1)S(1)}, u32[]{:S(2)}, u32[]{:S(2)}) collective-permute-start(bf16[128,512]{1,0:T(8,128)(2,1)S(1)} %get-tuple-element.19), channel_id=1, source_target_pairs={{0,8},{8,16},{16,24},{24,0},{1,9},{9,17},{17,25},{25,1},{2,10},{10... | collective-permute-start | bytes 393224 | tf_op jit(solution)/shard_map/ppermute | solution.py:19
Sparse Core Ops, SparseCore 0:
  74.1 33.8 reduce-scatter.2
  110.3 32.6 reduce-scatter.4
